TPU v7x, 256 devices: a whole 4x4x8 slice. The times are simulated.
256 devices in a mesh: dp: 32 (over z, y), row: 2 (over core), col: 4 (over x).
Axes of the slice: x: 4, y: 4, z: 8, core: 2. Of those that a mesh axis runs over, the one named last changes fastest.
Arguments:
- x_input: bfloat16 [32, 32, 64, 640], P('dp', 'row', 'col'), may hold values from -6 to 6
- pre_act: bfloat16 [32, 32, 64, 640], P('dp', 'row', 'col'), may hold values from -6 to 6
- out_grad: bfloat16 [32, 32, 64, 640], P('dp', 'row', 'col'), may hold values from -0.15625 to 0.15625
- conv_weight: bfloat16 [3, 3, 640, 640], replicated, may hold values from -0.078125 to 0.078125
- q_prev: float32 [5760, 2, 64], replicated, may hold values from -6 to 6
Outputs:
- p_basis: float32 [640, 2, 64], P('dp')
- q_next: float32 [5760, 2, 64], P('dp')
All inputs are finite; a program needn't handle non-finite values.
Results may differ from a plain program's by a relative error of at most 0.0036.
Values may be sent and summed in bfloat16 or wider, within the bound.
A program may use at most 128 MiB of HBM per device.

v0:
```python
import jax
import jax.numpy as jnp
from jax import lax
from jax.sharding import PartitionSpec as P


def padded_2(value, sides, width):
    for axis, dim in sides:
        size, length = (lax.axis_size(axis), value.shape[dim])
        up = [(i, (i + 1) % size) for i in range(size - 1)]
        down = [(j, i) for i, j in up]
        last = lax.slice_in_dim(value, length - width, length, axis=dim)
        leading = lax.slice_in_dim(value, 0, width, axis=dim)
        before = lax.ppermute(last, axis, up)
        after = lax.ppermute(leading, axis, down)
        value = jnp.concatenate([before, value, after], axis=dim)
    return value


def silu_slope(pre_float):
    sigma = jax.nn.sigmoid(pre_float)
    return sigma * (1.0 + pre_float * (1.0 - sigma))


def contract_first(left, right, exact):
    if exact:
        return lax.dot_general(
            left,
            right,
            (((0,), (0,)), ((), ())),
            precision=lax.Precision.HIGHEST,
            preferred_element_type=jnp.float32,
        )
    return lax.dot_general(
        left, right, (((0,), (0,)), ((), ())), preferred_element_type=jnp.float32
    )


def tap_window(padded, shift_row, shift_col, height, breadth):
    return padded[
        1 + shift_row : 1 + shift_row + height, 1 + shift_col : 1 + shift_col + breadth, :
    ].reshape(height * breadth, padded.shape[2])


def column_terms(moments, q_prev):
    return jnp.stack(
        [contract_first(moments[layer], q_prev[:, layer, :], True) for layer in range(2)], axis=1
    )


def row_terms(moments, ortho_basis):
    return jnp.stack(
        [
            jnp.dot(
                moments[layer],
                ortho_basis[:, layer, :],
                precision=lax.Precision.HIGHEST,
                preferred_element_type=jnp.float32,
            )
            for layer in range(2)
        ],
        axis=1,
    )


def gram_of(power_raw):
    return jnp.einsum(
        "mqn,mqg->qng",
        power_raw,
        power_raw,
        precision=lax.Precision.HIGHEST,
        preferred_element_type=jnp.float32,
    )


def orthonormal(power_raw, gram_matrix):
    bases = []
    for layer in range(2):
        lower = jnp.linalg.cholesky(gram_matrix[layer])
        bases.append(
            lax.linalg.triangular_solve(
                lower, power_raw[:, layer, :], left_side=False, lower=True, transpose_a=True
            )
        )
    return jnp.stack(bases, axis=1)


def on_device(x_input, pre_act, out_grad, conv_weight, q_prev):
    height, breadth, channels = (x_input.shape[1], x_input.shape[2], x_input.shape[3])
    pixels = height * breadth
    input_tile = x_input.reshape(height, breadth, channels)
    grad_tile = out_grad.reshape(height, breadth, channels)
    pre_float = pre_act.reshape(pixels, channels).astype(jnp.float32)
    hidden_flat = jax.nn.silu(pre_float).astype(jnp.bfloat16)
    grad_pad = padded_2(grad_tile, (("row", 0), ("col", 1)), 1)
    back_grad = jnp.zeros((pixels, channels), jnp.float32)
    second_taps = []
    for shift_row in (-1, 0, 1):
        for shift_col in (-1, 0, 1):
            window = tap_window(grad_pad, -shift_row, -shift_col, height, breadth)
            back_grad = back_grad + lax.dot_general(
                window,
                conv_weight[shift_row + 1, shift_col + 1],
                (((1,), (1,)), ((), ())),
                preferred_element_type=jnp.float32,
            )
            second_taps.append(contract_first(hidden_flat, window, False))
    pre_grad = (back_grad * silu_slope(pre_float)).astype(jnp.bfloat16)
    first_taps = []
    deriv_pad = padded_2(pre_grad.reshape(height, breadth, channels), (("row", 0), ("col", 1)), 1)
    input_flat = input_tile.reshape(pixels, channels)
    for shift_row in (-1, 0, 1):
        for shift_col in (-1, 0, 1):
            first_taps.append(
                contract_first(
                    input_flat,
                    tap_window(deriv_pad, -shift_row, -shift_col, height, breadth),
                    False,
                )
            )
    moments = jnp.stack(
        [
            jnp.stack(first_taps).reshape(9 * channels, channels),
            jnp.stack(second_taps).reshape(9 * channels, channels),
        ]
    )
    kernel_rows = moments.shape[1]
    owner = lax.axis_index("dp")
    basis_count = channels // lax.axis_size("dp")
    factor_count = kernel_rows // lax.axis_size("dp")
    power_raw = lax.psum(column_terms(moments, q_prev), ("dp", "row", "col"))
    ortho_basis = orthonormal(power_raw, gram_of(power_raw))
    factor_full = lax.psum(row_terms(moments, ortho_basis), ("dp", "row", "col"))
    basis_out = lax.dynamic_slice_in_dim(ortho_basis, owner * basis_count, basis_count, 0)
    factor_out = lax.dynamic_slice_in_dim(factor_full, owner * factor_count, factor_count, 0)
    return (basis_out, factor_out)


def solution(mesh):
    placed = (
        P("dp", "row", "col", None),
        P("dp", "row", "col", None),
        P("dp", "row", "col", None),
        P(),
        P(),
    )
    return jax.shard_map(
        on_device,
        mesh=mesh,
        in_specs=placed,
        out_specs=(P("dp", None, None), P("dp", None, None)),
        check_vma=False,
    )
```

profile of v0, /device:TPU:1, one launch (start us, length us, event | category | flops | bytes accessed | tf_op | source)
XLA Modules:
  0.0 653.8 jit_solution(3594010810887087729)
XLA Ops:
  8.0 5.1 collective-permute-start.1
  13.2 1.3 collective-permute-start
  17.9 1.4 collective-permute-start.3
  21.8 1.6 fusion.23
  24.1 1.3 maximum_maximum_fusion
  36.0 4.6 collective-permute-start.5
  40.6 1.5 collective-permute-start.4
  42.1 8.8 %fusion.12 = f32[640,1,64]{0,2,1:T(8,128)S(1)} fusion(f32[5760,640]{1,0:T(8,128)S(1)} %bitcast.253, f32[5760,2,64]{0,2,1:T(8,128)S(1)} %copy-done.5), kind=kOutput, calls=%fused_computation.38 | convolution fusion | flops 2831155200 | bytes 16384000 | tf_op jit(solution)/shard_map/dot_general | solution.py:27
  51.0 3.1 collective-permute-start.7
  54.2 1.5 collective-permute-start.6
  55.8 3.2 collective-permute-done.6
  63.7 9.2 %fusion.9 = f32[640,1,64]{0,2,1:T(8,128)S(1)} fusion(f32[5760,640]{1,0:T(8,128)S(1)} %bitcast.249, f32[5760,2,64]{0,2,1:T(8,128)S(1)} %copy-done.5), kind=kOutput, calls=%fused_computation.37 | convolution fusion | flops 2831155200 | bytes 16384000 | tf_op jit(solution)/shard_map/dot_general | solution.py:27
  73.8 249.9 %all-reduce.3.cloned.1.call-done = f32[640,2,64]{0,2,1:T(8,128)} async-done(((f32[640,2,64]{0,2,1:T(8,128)}), f32[640,2,64]{0,2,1:T(8,128)}) %all-reduce.3.cloned.1.call-update) | async-done | bytes 327696 | tf_op jit(solution)/shard_map/psum | solution.py:131
  323.7 1.5 fusion.62
  325.4 5.8 cholesky.44
  332.6 4.9 custom-call.6
  337.5 5.9 cholesky.55
  344.7 4.9 custom-call.7
  349.6 1.4 fusion.45
  351.1 17.3 %convolution_bitcast_fusion = f32[5760,1,64]{0,2,1:T(8,128)S(1)} fusion(f32[5760,640]{1,0:T(8,128)} %bitcast.254, f32[64,640]{1,0:T(8,128)S(1)} %fusion.45), kind=kOutput, calls=%fused_computation | convolution fusion | flops 2831155200 | bytes 16384000 | tf_op jit(solution)/shard_map/dot_general | solution.py:54
  368.8 14.2 %convolution_bitcast_fusion.1 = f32[5760,1,64]{0,2,1:T(8,128)S(1)} fusion(f32[5760,640]{1,0:T(8,128)S(1)} %bitcast.252, f32[64,640]{1,0:T(8,128)S(1)} %fusion.46), kind=kOutput, calls=%fused_computation.1 | convolution fusion | flops 2831155200 | bytes 16384000 | tf_op jit(solution)/shard_map/dot_general | solution.py:54
  383.0 1.8 pad_maximum_fusion
  385.6 259.4 %all-reduce.5.cloned.1.call-done = f32[5760,2,64]{0,2,1:T(8,128)} async-done(((f32[5760,2,64]{0,2,1:T(8,128)}), f32[5760,2,64]{0,2,1:T(8,128)}) %all-reduce.5.cloned.1.call-update) | async-done | bytes 2949136 | tf_op jit(solution)/shard_map/psum | solution.py:133
  645.1 1.7 constant_dynamic-slice_fusion
  (92 shorter events, 27.5 us)
Async XLA Ops:
  7.2 52.3 %copy-start = (bf16[1,16,16,640]{3,2,1,0:T(8,128)(2,1)S(1)}, bf16[1,16,16,640]{3,2,1,0:T(8,128)(2,1)}, u32[]{:S(2)}) copy-start(bf16[1,16,16,640]{3,2,1,0:T(8,128)(2,1)} %param.8) | copy-start | bytes 983044
  7.2 316.5 %all-reduce.3.cloned.1.call-start = ((), (), s32[]{:S(2)}) async-start(), calls=%async_computation | async-start | bytes 655360 | tf_op jit(solution)/shard_map/psum | solution.py:131
  8.0 8.8 %collective-permute-start.1 = (bf16[1,16,640]{2,1,0:T(8,128)(2,1)S(1)}, bf16[1,16,640]{2,1,0:T(8,128)(2,1)S(1)}, u32[]{:S(2)}, u32[]{:S(2)}) collective-permute-start(bf16[1,16,640]{2,1,0:T(8,128)(2,1)S(1)} %get-tuple-element.33), channel_id=1, source_target_pairs={{4,0},{5,1},{6,2},{7,3},{12,8},{13,9},{14,10},{15,11},{20,16},{21,... | collective-permute-start | bytes 61448 | tf_op jit(solution)/shard_map/ppermute | solution.py:15
  13.2 3.7 collective-permute-start
  17.9 5.5 collective-permute-start.3
  19.3 4.8 collective-permute-start.2
  23.4 4.1 copy-start.3
  23.4 4.1 copy-start.6
  27.0 2.2 slice-start.4
  27.5 2.8 slice-start.5
  32.7 9.4 %copy-start.2 = (f32[9,640,640]{2,1,0:T(8,128)}, f32[9,640,640]{2,1,0:T(8,128)S(1)}, u32[]{:S(2)}) copy-start(f32[9,640,640]{2,1,0:T(8,128)S(1)} %bitcast_dynamic-update-slice_fusion.9) | copy-start | bytes 44236804
  33.2 8.9 %copy-start.5 = (f32[5760,2,64]{0,2,1:T(8,128)S(1)}, f32[5760,2,64]{0,2,1:T(8,128)}, u32[]{:S(2)}) copy-start(f32[5760,2,64]{0,2,1:T(8,128)} %param.12) | copy-start | bytes 8847364
  36.0 14.9 %collective-permute-start.5 = (bf16[1,16,640]{2,1,0:T(8,128)(2,1)S(1)}, bf16[1,16,640]{2,1,0:T(8,128)(2,1)S(1)}, u32[]{:S(2)}, u32[]{:S(2)}) collective-permute-start(bf16[1,16,640]{2,1,0:T(8,128)(2,1)S(1)} %get-tuple-element.29), channel_id=1, source_target_pairs={{4,0},{5,1},{6,2},{7,3},{12,8},{13,9},{14,10},{15,11},{20,16},{21,... | collective-permute-start | bytes 61448 | tf_op jit(solution)/shard_map/ppermute | solution.py:15
  40.6 10.3 %collective-permute-start.4 = (bf16[1,16,640]{2,1,0:T(8,128)(2,1)S(1)}, bf16[1,16,640]{2,1,0:T(8,128)(2,1)S(1)}, u32[]{:S(2)}, u32[]{:S(2)}) collective-permute-start(bf16[1,16,640]{2,1,0:T(8,128)(2,1)S(1)} %get-tuple-element.28), channel_id=1, source_target_pairs={{0,4},{1,5},{2,6},{3,7},{8,12},{9,13},{10,14},{11,15},{16,20},{17,... | collective-permute-start | bytes 61448 | tf_op jit(solution)/shard_map/ppermute | solution.py:14
  51.0 4.7 collective-permute-start.7
  54.2 4.8 collective-permute-start.6
  63.7 9.2 %copy-start.1 = (f32[9,640,640]{2,1,0:T(8,128)}, f32[9,640,640]{2,1,0:T(8,128)S(1)}, u32[]{:S(2)}) copy-start(f32[9,640,640]{2,1,0:T(8,128)S(1)} %bitcast_dynamic-update-slice_fusion) | copy-start | bytes 44236804
  73.7 571.4 %all-reduce.5.cloned.1.call-start = ((), (), s32[]{:S(2)}) async-start(), calls=%async_computation.1 | async-start | bytes 5898240 | tf_op jit(solution)/shard_map/psum | solution.py:133
  349.6 19.1 %slice-start = ((s8[14745600]{0:T(1024)(128)(4,1)}), s8[4194304]{0:T(1024)(128)(4,1)S(1)}, s32[]{:S(2)}) async-start(s8[14745600]{0:T(1024)(128)(4,1)} %bitcast.250), calls=%async_computation.2 | async-start | bytes 8388608
  351.0 17.3 %copy-start.4 = (f32[640,2,64]{0,2,1:T(8,128)S(1)}, f32[640,2,64]{0,2,1:T(8,128)}, u32[]{:S(2)}) copy-start(f32[640,2,64]{0,2,1:T(8,128)} %all-reduce.3.cloned.1.call-done) | copy-start | bytes 983044
  351.0 17.7 %slice-start.1 = ((s8[14745600]{0:T(1024)(128)(4,1)}), s8[4194304]{0:T(1024)(128)(4,1)S(1)}, s32[]{:S(2)}) async-start(s8[14745600]{0:T(1024)(128)(4,1)} %bitcast.250), calls=%async_computation.3 | async-start | bytes 8388608
  351.1 17.7 %slice-start.2 = ((s8[14745600]{0:T(1024)(128)(4,1)}), s8[4194304]{0:T(1024)(128)(4,1)S(1)}, s32[]{:S(2)}) async-start(s8[14745600]{0:T(1024)(128)(4,1)} %bitcast.250), calls=%async_computation.4 | async-start | bytes 8388608
  351.1 17.7 %slice-start.3 = ((s8[14745600]{0:T(1024)(128)(4,1)}), s8[2162688]{0:T(1024)(128)(4,1)S(1)}, s32[]{:S(2)}) async-start(s8[14745600]{0:T(1024)(128)(4,1)} %bitcast.250), calls=%async_computation.5 | async-start | bytes 4325376
Sparse Core Ops, SparseCore 0:
  73.8 249.7 all-reduce.2
  385.0 260.0 all-reduce.4
where the time goes:
time: 662 us; the launch traced here: 654 us
  waiting for transfers between devices  513 us (77%)
  matrix products  66.6 us (10%)
  other arithmetic  33.1 us (5%)
  starting transfers between devices  19.9 us (3%)
  between operations  14.8 us (2%)
    psum x1, waiting for transfers between devices, on_device(): lax.psum(row_terms(moments, ortho_basis), ('dp', 'row', 'col'))  259 us
    psum x1, waiting for transfers between devices, on_device(): power_raw = lax.psum(column_terms(moments, q_prev), ('dp', 'row', 'col'))  250 us
    dot_general x2, matrix products, row_terms(): jnp.dot(moments[layer], ortho_basis[:, layer, :], precision=lax.Precision...  31.5 us
    dot_general x2, matrix products, contract_first(): lax.dot_general(left, right, (((0,), (0,)), ((), ())), precision=lax.Prec...  18.1 us
  transfers between devices with their start and end apart: 10, of which 4 were waited for; matrix products, arithmetic and copies ran while one was open for 2% of the time, Pallas kernels for 0%

commit v1 on v0

--- a/solution.py
+++ b/solution.py
@@ -128,11 +128,14 @@
     owner = lax.axis_index("dp")
     basis_count = channels // lax.axis_size("dp")
     factor_count = kernel_rows // lax.axis_size("dp")
-    power_raw = lax.psum(column_terms(moments, q_prev), ("dp", "row", "col"))
+    power_raw = column_terms(moments, q_prev)
+    for axis in ("row", "col", "dp"):
+        power_raw = lax.psum(power_raw, axis)
     ortho_basis = orthonormal(power_raw, gram_of(power_raw))
-    factor_full = lax.psum(row_terms(moments, ortho_basis), ("dp", "row", "col"))
+    factor_out = lax.psum_scatter(row_terms(moments, ortho_basis), "dp", scatter_dimension=0, tiled=True)
+    for axis in ("row", "col"):
+        factor_out = lax.psum(factor_out, axis)
     basis_out = lax.dynamic_slice_in_dim(ortho_basis, owner * basis_count, basis_count, 0)
-    factor_out = lax.dynamic_slice_in_dim(factor_full, owner * factor_count, factor_count, 0)
     return (basis_out, factor_out)
 
 

time: 662 us -> 616 us (0.931)
  waiting for transfers between devices: 513 us -> 465 us
    psum x2 -> x5, waiting for transfers between devices: 509 us -> 307 us  [the longest x3 229 us: on_device(): power_raw = lax.psum(power_raw, axis)]
    unnamed x2 -> x7, waiting for transfers between devices: 0.03 us -> 155 us
  transfers between devices with their start and end apart: 10 -> 14, of which waited for: 4 -> 8; matrix products, arithmetic and copies ran while one was open for 2% -> 3% of each run, Pallas kernels for 0% -> 0%
where the time goes in v1:
time: 616 us; the launch traced here: 609 us
  waiting for transfers between devices  465 us (75%)
  matrix products  66.6 us (11%)
  other arithmetic  33.1 us (5%)
  starting transfers between devices  20 us (3%)
  between operations  15.6 us (3%)
  local copies, waits for them, and re-layouts  8.22 us (1%)
    psum x3, waiting for transfers between devices, on_device(): power_raw = lax.psum(power_raw, axis)  229 us
    unnamed x7, waiting for transfers between devices  155 us
    psum x2, waiting for transfers between devices, on_device(): factor_out = lax.psum(factor_out, axis)  78 us
    dot_general x2, matrix products, row_terms(): jnp.dot(moments[layer], ortho_basis[:, layer, :], precision=lax.Precision...  31.5 us
    dot_general x2, matrix products, contract_first(): lax.dot_general(left, right, (((0,), (0,)), ((), ())), precision=lax.Prec...  18.1 us
    another operation x6, other arithmetic, orthonormal(): lower = jnp.linalg.cholesky(gram_matrix[layer])  13.1 us
    ppermute x4, starting transfers between devices, padded_2(): after = lax.ppermute(leading, axis, down)  12.5 us
  transfers between devices with their start and end apart: 14, of which 8 were waited for; matrix products, arithmetic and copies ran while one was open for 3% of the time, Pallas kernels for 0%

profile of v1, /device:TPU:1, one launch (start us, length us, event | category | flops | bytes accessed | tf_op | source)
XLA Modules:
  0.0 608.6 jit_solution(7711296566547497687)
XLA Ops:
  8.0 5.1 collective-permute-start.1
  21.8 1.6 fusion.23
  36.0 4.6 collective-permute-start.5
  42.1 8.8 %fusion.12 = f32[640,1,64]{0,2,1:T(8,128)S(1)} fusion(f32[5760,640]{1,0:T(8,128)S(1)} %bitcast.256, f32[5760,2,64]{0,2,1:T(8,128)S(1)} %copy-done.6), kind=kOutput, calls=%fused_computation.38 | convolution fusion | flops 2831155200 | bytes 16384000 | tf_op jit(solution)/shard_map/dot_general | solution.py:27
  51.1 3.1 collective-permute-start.7
  54.2 1.5 collective-permute-start.6
  55.8 3.2 collective-permute-done.6
  63.7 9.3 %fusion.9 = f32[640,1,64]{0,2,1:T(8,128)S(1)} fusion(f32[5760,640]{1,0:T(8,128)S(1)} %bitcast.252, f32[5760,2,64]{0,2,1:T(8,128)S(1)} %copy-done.6), kind=kOutput, calls=%fused_computation.37 | convolution fusion | flops 2831155200 | bytes 16384000 | tf_op jit(solution)/shard_map/dot_general | solution.py:27
  73.8 33.9 %all-reduce.8.cloned.1.call-done = f32[640,2,64]{0,2,1:T(8,128)} async-done(((f32[640,2,64]{0,2,1:T(8,128)}), f32[640,2,64]{0,2,1:T(8,128)}) %all-reduce.8.cloned.1.call-update) | async-done | bytes 327696 | tf_op jit(solution)/shard_map/psum | solution.py:133
  107.7 47.9 %all-reduce.10.cloned.1.call-done = f32[640,2,64]{0,2,1:T(8,128)} async-done(((f32[640,2,64]{0,2,1:T(8,128)}), f32[640,2,64]{0,2,1:T(8,128)}) %all-reduce.10.cloned.1.call-update) | async-done | bytes 327696 | tf_op jit(solution)/shard_map/psum | solution.py:133
  155.7 146.8 %all-reduce.12.cloned.1.call-done = f32[640,2,64]{0,2,1:T(8,128)} async-done(((f32[640,2,64]{0,2,1:T(8,128)}), f32[640,2,64]{0,2,1:T(8,128)}) %all-reduce.12.cloned.1.call-update) | async-done | bytes 327696 | tf_op jit(solution)/shard_map/psum | solution.py:133
  302.5 1.5 fusion.62
  304.2 5.8 cholesky.44
  311.4 4.9 custom-call.6
  316.3 5.9 cholesky.55
  323.5 4.9 custom-call.7
  329.9 17.3 %convolution_bitcast_fusion = f32[5760,1,64]{0,2,1:T(8,128)S(1)} fusion(f32[5760,640]{1,0:T(8,128)} %bitcast.257, f32[64,640]{1,0:T(8,128)S(1)} %fusion.45), kind=kOutput, calls=%fused_computation | convolution fusion | flops 2831155200 | bytes 16384000 | tf_op jit(solution)/shard_map/dot_general | solution.py:54
  347.6 14.2 %convolution_bitcast_fusion.1 = f32[5760,1,64]{0,2,1:T(8,128)S(1)} fusion(f32[5760,640]{1,0:T(8,128)S(1)} %bitcast.255, f32[64,640]{1,0:T(8,128)S(1)} %fusion.46), kind=kOutput, calls=%fused_computation.1 | convolution fusion | flops 2831155200 | bytes 16384000 | tf_op jit(solution)/shard_map/dot_general | solution.py:54
  361.8 1.8 pad_maximum_fusion
  365.0 154.5 %all-reduce.18.cloned.1.call-done = f32[5760,2,64]{0,2,1:T(8,128)} async-done(((f32[5760,2,64]{0,2,1:T(8,128)}), f32[5760,2,64]{0,2,1:T(8,128)}) %all-reduce.18.cloned.1.call-update) | async-done | bytes 2949136
  519.5 1.7 constant_dynamic-slice_fusion
  521.2 31.8 %all-reduce.14.cloned.1.call-done = f32[180,2,64]{0,2,1:T(8,128)} async-done(((f32[180,2,64]{0,2,1:T(8,128)}), f32[180,2,64]{0,2,1:T(8,128)}) %all-reduce.14.cloned.1.call-update) | async-done | bytes 92176 | tf_op jit(solution)/shard_map/psum | solution.py:137
  553.8 46.2 %all-reduce.16.cloned.1.call-done = f32[180,2,64]{0,2,1:T(8,128)} async-done(((f32[180,2,64]{0,2,1:T(8,128)}), f32[180,2,64]{0,2,1:T(8,128)}) %all-reduce.16.cloned.1.call-update) | async-done | bytes 92176 | tf_op jit(solution)/shard_map/psum | solution.py:137
  600.0 1.6 copy.42
  (110 shorter events, 35.1 us)
Async XLA Ops:
  7.2 52.3 %copy-start = (bf16[1,16,16,640]{3,2,1,0:T(8,128)(2,1)S(1)}, bf16[1,16,16,640]{3,2,1,0:T(8,128)(2,1)}, u32[]{:S(2)}) copy-start(bf16[1,16,16,640]{3,2,1,0:T(8,128)(2,1)} %param.8) | copy-start | bytes 983044
  7.2 100.5 %all-reduce.8.cloned.1.call-start = ((), (), s32[]{:S(2)}) async-start(), calls=%async_computation | async-start | bytes 655360 | tf_op jit(solution)/shard_map/psum | solution.py:133
  8.0 8.8 %collective-permute-start.1 = (bf16[1,16,640]{2,1,0:T(8,128)(2,1)S(1)}, bf16[1,16,640]{2,1,0:T(8,128)(2,1)S(1)}, u32[]{:S(2)}, u32[]{:S(2)}) collective-permute-start(bf16[1,16,640]{2,1,0:T(8,128)(2,1)S(1)} %get-tuple-element.35), channel_id=1, source_target_pairs={{4,0},{5,1},{6,2},{7,3},{12,8},{13,9},{14,10},{15,11},{20,16},{21,... | collective-permute-start | bytes 61448 | tf_op jit(solution)/shard_map/ppermute | solution.py:15
  13.2 3.7 collective-permute-start
  17.9 5.5 collective-permute-start.3
  19.3 4.8 collective-permute-start.2
  32.7 9.4 %copy-start.3 = (f32[9,640,640]{2,1,0:T(8,128)}, f32[9,640,640]{2,1,0:T(8,128)S(1)}, u32[]{:S(2)}) copy-start(f32[9,640,640]{2,1,0:T(8,128)S(1)} %bitcast_dynamic-update-slice_fusion.9) | copy-start | bytes 44236804
  33.2 9.0 %copy-start.6 = (f32[5760,2,64]{0,2,1:T(8,128)S(1)}, f32[5760,2,64]{0,2,1:T(8,128)}, u32[]{:S(2)}) copy-start(f32[5760,2,64]{0,2,1:T(8,128)} %param.12) | copy-start | bytes 8847364
  36.0 14.9 %collective-permute-start.5 = (bf16[1,16,640]{2,1,0:T(8,128)(2,1)S(1)}, bf16[1,16,640]{2,1,0:T(8,128)(2,1)S(1)}, u32[]{:S(2)}, u32[]{:S(2)}) collective-permute-start(bf16[1,16,640]{2,1,0:T(8,128)(2,1)S(1)} %get-tuple-element.31), channel_id=1, source_target_pairs={{4,0},{5,1},{6,2},{7,3},{12,8},{13,9},{14,10},{15,11},{20,16},{21,... | collective-permute-start | bytes 61448 | tf_op jit(solution)/shard_map/ppermute | solution.py:15
  40.6 10.3 %collective-permute-start.4 = (bf16[1,16,640]{2,1,0:T(8,128)(2,1)S(1)}, bf16[1,16,640]{2,1,0:T(8,128)(2,1)S(1)}, u32[]{:S(2)}, u32[]{:S(2)}) collective-permute-start(bf16[1,16,640]{2,1,0:T(8,128)(2,1)S(1)} %get-tuple-element.30), channel_id=1, source_target_pairs={{0,4},{1,5},{2,6},{3,7},{8,12},{9,13},{10,14},{11,15},{16,20},{17,... | collective-permute-start | bytes 61448 | tf_op jit(solution)/shard_map/ppermute | solution.py:14
  51.1 4.7 collective-permute-start.7
  54.2 4.8 collective-permute-start.6
  63.7 9.3 %copy-start.2 = (f32[9,640,640]{2,1,0:T(8,128)}, f32[9,640,640]{2,1,0:T(8,128)S(1)}, u32[]{:S(2)}) copy-start(f32[9,640,640]{2,1,0:T(8,128)S(1)} %bitcast_dynamic-update-slice_fusion) | copy-start | bytes 44236804
  73.7 81.9 %all-reduce.10.cloned.1.call-start = ((), (), s32[]{:S(2)}) async-start(), calls=%async_computation.1 | async-start | bytes 655360 | tf_op jit(solution)/shard_map/psum | solution.py:133
  107.7 194.8 %all-reduce.12.cloned.1.call-start = ((), (), s32[]{:S(2)}) async-start(), calls=%async_computation.2 | async-start | bytes 655360 | tf_op jit(solution)/shard_map/psum | solution.py:133
  155.7 363.8 %all-reduce.18.cloned.1.call-start = ((), (), s32[]{:S(2)}) async-start(), calls=%async_computation.5 | async-start | bytes 5898240
  328.4 19.1 %slice-start = ((s8[14745600]{0:T(1024)(128)(4,1)}), s8[4194304]{0:T(1024)(128)(4,1)S(1)}, s32[]{:S(2)}) async-start(s8[14745600]{0:T(1024)(128)(4,1)} %bitcast.253), calls=%async_computation.6 | async-start | bytes 8388608
  329.8 17.3 %copy-start.5 = (f32[640,2,64]{0,2,1:T(8,128)S(1)}, f32[640,2,64]{0,2,1:T(8,128)}, u32[]{:S(2)}) copy-start(f32[640,2,64]{0,2,1:T(8,128)} %all-reduce.12.cloned.1.call-done) | copy-start | bytes 983044
  329.9 17.7 %slice-start.1 = ((s8[14745600]{0:T(1024)(128)(4,1)}), s8[4194304]{0:T(1024)(128)(4,1)S(1)}, s32[]{:S(2)}) async-start(s8[14745600]{0:T(1024)(128)(4,1)} %bitcast.253), calls=%async_computation.7 | async-start | bytes 8388608
  329.9 17.7 %slice-start.2 = ((s8[14745600]{0:T(1024)(128)(4,1)}), s8[4194304]{0:T(1024)(128)(4,1)S(1)}, s32[]{:S(2)}) async-start(s8[14745600]{0:T(1024)(128)(4,1)} %bitcast.253), calls=%async_computation.8 | async-start | bytes 8388608
  329.9 17.7 %slice-start.3 = ((s8[14745600]{0:T(1024)(128)(4,1)}), s8[2162688]{0:T(1024)(128)(4,1)S(1)}, s32[]{:S(2)}) async-start(s8[14745600]{0:T(1024)(128)(4,1)} %bitcast.253), calls=%async_computation.9 | async-start | bytes 4325376
  347.6 254.0 %copy-start.1 = (bf16[1,16,16,640]{3,2,1,0:T(8,128)(2,1)S(1)}, bf16[1,16,16,640]{3,2,1,0:T(8,128)(2,1)}, u32[]{:S(2)}) copy-start(bf16[1,16,16,640]{3,2,1,0:T(8,128)(2,1)} %param.8) | copy-start | bytes 983044
  363.7 189.3 %all-reduce.14.cloned.1.call-start = ((), (), s32[]{:S(2)}) async-start(), calls=%async_computation.3 | async-start | bytes 262144 | tf_op jit(solution)/shard_map/psum | solution.py:137
  521.2 78.9 %all-reduce.16.cloned.1.call-start = ((), (), s32[]{:S(2)}) async-start(), calls=%async_computation.4 | async-start | bytes 262144 | tf_op jit(solution)/shard_map/psum | solution.py:137
  (5 other events, 15.2 us)
Sparse Core Ops, SparseCore 0:
  73.8 33.7 all-reduce.7
  110.1 45.5 all-reduce.9
  159.5 142.9 all-reduce.11
  363.8 155.6 all-reduce.17
  522.6 30.3 all-reduce.13
  555.3 44.7 all-reduce.15
